TPU v7x, 1024 devices: a whole 8x8x8 slice. The times are simulated.
1024 devices in a mesh: pole: 8 (over x), row: 16 (over y, z_lo), col: 8 (over z_hi, core).
Axes of the slice: x: 8, y: 8, z: 8 (z_hi: 4, z_lo: 2; z = z_hi * 2 + z_lo), core: 2. Of those that a mesh axis runs over, the one named last changes fastest.
Arguments:
- factor: float32 [8, 2, 512, 16, 128], P('pole', None, 'row'), may hold values from -0.375 to 0.375
- green: float32 [8, 2, 512, 512], P('pole', None, 'row', 'col'), may hold values from -6 to 6
- diag_inv: float32 [8, 2, 16, 128, 128], P('pole', None, 'row'), may hold values from -6 to 6
- pole_weight: float32 [8, 2], P('pole'), may hold values from -4 to 4
- structure: int32 [16, 8], replicated, may hold values 0 or 1
- widths: int32 [16], replicated, may hold values from 32 to 128, as said below
Outputs:
- density_off: float32 [16, 128, 512], P('row', None, 'col')
- density_diag: float32 [16, 128, 128], P('row')
Inputs may be any that keep to these rules, and one draw needn't show every extreme that they name: `widths`: some supernode has all 128 columns.
All inputs are finite; a program needn't handle non-finite values.
Results may differ from a plain program's by a relative error of at most 0.0001.
Values sent between devices are 32-bit elements; how exact they have to be, the bound alone decides.
No kernel may reach another device: no remote copies, remote signals or barrier semaphores. Data moves between devices by JAX's collectives and lax.ppermute only.
A program may use at most 32 MiB of HBM per device.

v0:
```python
import jax
import jax.numpy as jnp
from jax import lax
from jax.sharding import PartitionSpec as P

highest = lax.Precision.HIGHEST


def contract(form, left, right):
    return jnp.einsum(form, left, right, precision=highest, preferred_element_type=jnp.float32)


def offdiag_term(lower_part, green_part):
    real_part = contract("akw,ac->kwc", lower_part[1], green_part[1]) - contract(
        "akw,ac->kwc", lower_part[0], green_part[0]
    )
    imag_part = -(
        contract("akw,ac->kwc", lower_part[0], green_part[1])
        + contract("akw,ac->kwc", lower_part[1], green_part[0])
    )
    return jnp.stack([real_part, imag_part], axis=1)


def diag_product(row_inv, lower_cols):
    real_part = contract("kwc,ckv->kwv", row_inv[:, 0], lower_cols[0]) - contract(
        "kwc,ckv->kwv", row_inv[:, 1], lower_cols[1]
    )
    imag_part = contract("kwc,ckv->kwv", row_inv[:, 0], lower_cols[1]) + contract(
        "kwc,ckv->kwv", row_inv[:, 1], lower_cols[0]
    )
    return (real_part, imag_part)


def per_device(factor, green, diag_inv, pole_weight, structure, widths):
    row_count = lax.axis_size("row")
    row_index = lax.axis_index("row")
    col_index = lax.axis_index("col")
    rows_here = factor.shape[2]
    node_count = factor.shape[3]
    node_width = factor.shape[4]
    cols_here = green.shape[3]
    nodes_here = node_count // row_count
    block_rows = rows_here * row_count // structure.shape[1]
    mask_rows = jnp.repeat(structure.astype(jnp.float32), block_rows, axis=1)
    mask_cols = (jnp.arange(node_width)[None, :] < widths[:, None]).astype(jnp.float32)
    rows_local = lax.dynamic_slice_in_dim(mask_rows, row_index * rows_here, rows_here, 1)
    lower_here = factor[0] * rows_local.T[None, :, :, None] * mask_cols[None, None, :, :]
    row_inv = lax.psum_scatter(
        offdiag_term(lower_here, green[0]), "row", scatter_dimension=0, tiled=True
    )
    received = lax.all_to_all(lower_here, "row", split_axis=2, concat_axis=1, tiled=True)
    lower_cols = lax.dynamic_slice_in_dim(received, col_index * cols_here, cols_here, 1)
    real_weight = pole_weight[0, 0]
    imag_weight = pole_weight[0, 1]
    real_part, imag_part = diag_product(row_inv, lower_cols)
    first_col = (col_index == 0).astype(jnp.float32)
    cols_mine = lax.dynamic_slice_in_dim(mask_cols, row_index * nodes_here, nodes_here, 0)
    diag_mask = cols_mine[:, :, None] * cols_mine[:, None, :]
    diag_term = (
        real_weight * (first_col * diag_inv[0, 1] - imag_part)
        + imag_weight * (first_col * diag_inv[0, 0] - real_part)
    ) * diag_mask
    rows_mine = lax.dynamic_slice(
        mask_rows, (row_index * nodes_here, col_index * cols_here), (nodes_here, cols_here)
    )
    off_term = (
        (real_weight * row_inv[:, 1] + imag_weight * row_inv[:, 0])
        * cols_mine[:, :, None]
        * rows_mine[:, None, :]
    )
    density_diag = lax.psum(diag_term, ("pole", "col"))
    density_off = lax.psum(off_term, "pole")
    return (density_off, density_diag)


def solution(mesh):
    placed = (
        P("pole", None, "row", None, None),
        P("pole", None, "row", "col"),
        P("pole", None, "row", None, None),
        P("pole", None),
        P(),
        P(),
    )
    return jax.shard_map(
        per_device,
        mesh=mesh,
        in_specs=placed,
        out_specs=(P("row", None, "col"), P("row", None, None)),
        check_vma=False,
    )
```

profile of v0, /device:TPU:1, one launch (start us, length us, event | category | flops | bytes accessed | tf_op | source)
XLA Modules:
  0.0 688.2 jit_solution(5790289082018655073)
XLA Ops:
  7.2 0.0 all-reduce.6.cloned.1.call-start
  7.2 0.0 copy-start.2
  7.2 0.7 copy-done.2
  7.9 0.0 copy-start.4
  7.9 0.1 copy.14
  8.0 0.6 copy-done.4
  8.6 0.1 fusion.32
  8.6 0.1 broadcast_in_dim.2
  8.7 0.1 reshape.175
  8.8 0.1 dynamic-slice_bitcast_fusion.6
  8.9 0.0 copy-start.1
  8.9 1.3 fusion.10
  10.1 0.0 copy-done.1
  10.1 0.6 fusion.12
  10.8 0.6 fusion.11
  11.4 0.6 fusion.1
  12.0 0.6 fusion.2
  12.7 1.1 pad_maximum_fusion
  13.8 0.0 all-reduce.6.cloned.1.call-update
  13.8 0.8 copy.15
  14.7 10.9 %all-to-all-start = ((f32[2,32,16,128]{3,1,0,2:T(8,128)}), f32[2,32,16,128]{3,1,0,2:T(8,128)S(1)}, u32[]{:S(2)}, u32[]{:S(2)}) async-start(f32[2,32,16,128]{3,1,0,2:T(8,128)} %copy.15), calls=%async_computation | async-start | bytes 1048576 | tf_op jit(solution)/shard_map/all_to_all | solution.py:51
  25.6 0.0 all-reduce.4.cloned.1.call-start
  25.6 1.3 dynamic-slice
  26.9 0.0 copy-start.3
  26.9 0.1 dynamic-slice_bitcast_fusion.7
  27.0 0.6 copy-done.3
  27.6 0.7 fusion.42
  28.2 9.2 %all-to-all-done = f32[2,32,16,128]{3,1,0,2:T(8,128)S(1)} async-done(((f32[2,32,16,128]{3,1,0,2:T(8,128)}), f32[2,32,16,128]{3,1,0,2:T(8,128)S(1)}, u32[]{:S(2)}, u32[]{:S(2)}) %all-to-all-start) | async-done | bytes 524320 | tf_op jit(solution)/shard_map/all_to_all | solution.py:51
  37.5 131.1 %all-reduce.6.cloned.1.call-done = f32[16,2,128,64]{2,3,0,1:T(8,128)} async-done(((f32[16,2,128,64]{2,3,0,1:T(8,128)}), f32[16,2,128,64]{2,3,0,1:T(8,128)}) %all-reduce.6.cloned.1.call-update) | async-done | bytes 1048592
  168.6 0.0 copy-start
  168.6 1.7 fusion.15
  170.3 1.7 fusion.17
  172.0 0.0 copy-done
  172.1 2.3 fusion.7
  174.4 3.0 fusion.9
  177.4 0.0 all-reduce.4.cloned.1.call-update
  177.4 2.8 fusion.19
  180.3 23.0 %psum.14 = f32[1,128,64]{1,2,0:T(8,128)} all-reduce(f32[1,128,64]{1,2,0:T(8,128)S(1)} %fusion.19), channel_id=1, replica_groups=mesh['pole'=8,'row'=16,'col'=8] {'pole'}, use_global_device_ids=true, to_apply=%region_1.0 | all-reduce | flops 8192 | bytes 65536 | tf_op jit(solution)/shard_map/psum | solution.py:72
  203.2 476.7 %all-reduce.4.cloned.1.call-done = f32[1,128,128]{2,1,0:T(8,128)} async-done(((f32[1,128,128]{2,1,0:T(8,128)}), f32[1,128,128]{2,1,0:T(8,128)}) %all-reduce.4.cloned.1.call-update) | async-done | bytes 65552 | tf_op jit(solution)/shard_map/psum | solution.py:71
  679.9 1.5 copy.22
  (3 shorter events, 0.0 us)
Async XLA Ops:
  7.2 161.4 %all-reduce.6.cloned.1.call-start = ((), (), s32[]{:S(2)}) async-start(), calls=%async_computation.2 | async-start | bytes 2097152
  7.2 0.7 copy-start.2
  7.9 0.7 copy-start.4
  8.9 1.3 copy-start.1
  14.7 22.8 %all-to-all-start = ((f32[2,32,16,128]{3,1,0,2:T(8,128)}), f32[2,32,16,128]{3,1,0,2:T(8,128)S(1)}, u32[]{:S(2)}, u32[]{:S(2)}) async-start(f32[2,32,16,128]{3,1,0,2:T(8,128)} %copy.15), calls=%async_computation | async-start | bytes 1048576 | tf_op jit(solution)/shard_map/all_to_all | solution.py:51
  25.6 654.4 %all-reduce.4.cloned.1.call-start = ((), (), s32[]{:S(2)}) async-start(), calls=%async_computation.1 | async-start | bytes 131072 | tf_op jit(solution)/shard_map/psum | solution.py:71
  26.9 0.7 copy-start.3
  168.6 3.4 copy-start
Sparse Core Ops, SparseCore 0:
  13.9 154.6 all-reduce.5
  177.6 502.3 all-reduce.3
where the time goes:
time: 689 us; the launch traced here: 688 us
  waiting for transfers between devices  617 us (90%)
  blocking collectives  23 us (3%)
  between operations  14.2 us (2%)
  matrix products  11.3 us (2%)
  starting transfers between devices  11 us (2%)
    psum x1, waiting for transfers between devices, per_device(): density_diag = lax.psum(diag_term, ('pole', 'col'))  477 us
    unnamed x3, waiting for transfers between devices  131 us
    psum x1, blocking collectives, per_device(): density_off = lax.psum(off_term, 'pole')  23 us
  transfers between devices with their start and end apart: 3, of which 3 were waited for; matrix products, arithmetic and copies ran while one was open for 1% of the time, Pallas kernels for 0%

commit v1 on v0

v1 whole, which is shorter than its diff:
```python
import jax
import jax.numpy as jnp
from jax import lax
from jax.experimental import pallas as pl
from jax.experimental.pallas import tpu as pltpu
from jax.sharding import PartitionSpec as P

VMEM = pl.BlockSpec(memory_space=pltpu.VMEM)
SMEM = pl.BlockSpec(memory_space=pltpu.SMEM)


def split(value):
    high = value.astype(jnp.bfloat16)
    return high, (value - high.astype(jnp.float32)).astype(jnp.bfloat16)


def product(left, right):
    left_high, left_low = split(left)
    right_high, right_low = split(right)

    def one(a, b):
        return lax.dot_general(a, b, (((0,), (0,)), ((), ())), preferred_element_type=jnp.float32)

    return one(left_high, right_high) + (one(left_high, right_low) + one(left_low, right_high))


def compute(cols_here, rows_here, block_rows, poles, held, inverse, weight, structure, widths, sent):
    node = lax.axis_index("row")
    col = lax.axis_index("col")
    owners = held.shape[0]
    width = held.shape[2]
    real_weight, imag_weight = weight[0, 0], weight[0, 1]

    def present(block):
        return structure[block, node].astype(jnp.float32)

    green = jnp.concatenate(
        [held[r, 2 * rows_here :, :] * present(r * rows_here // block_rows) for r in range(owners)], axis=0
    )
    lower = jnp.concatenate(
        [
            held[:, :rows_here, :].reshape(owners * rows_here, width),
            held[:, rows_here : 2 * rows_here, :].reshape(owners * rows_here, width),
        ],
        axis=1,
    )
    parts = product(green, lower)
    real_part = parts[cols_here:, width:] - parts[:cols_here, :width]
    imag_part = -(parts[cols_here:, :width] + parts[:cols_here, width:])
    keep_lane = (lax.broadcasted_iota(jnp.int32, (cols_here, width), 1) < widths[node]).astype(jnp.float32)
    here = present(col * cols_here // block_rows)
    off_term = (real_weight * imag_part + imag_weight * real_part) * keep_lane * here
    other = (real_weight * real_part - imag_weight * imag_part) * keep_lane * here
    span = cols_here // rows_here
    rows = held[pl.ds(col * span, span), : 2 * rows_here, :]
    lower_cols = jnp.concatenate(
        [rows[:, :rows_here].reshape(cols_here, width), rows[:, rows_here:].reshape(cols_here, width)], axis=0
    )
    diag = product(jnp.concatenate([off_term, other], axis=0), lower_cols)
    first = (col == 0).astype(jnp.float32)
    keep = (lax.broadcasted_iota(jnp.int32, (width, width), 1) < widths[node]) & (
        lax.broadcasted_iota(jnp.int32, (width, width), 0) < widths[node]
    )
    diag = (first * (real_weight * inverse[1] + imag_weight * inverse[0]) - diag) * keep.astype(jnp.float32)
    diag_rows, off_rows = width // poles, cols_here // poles
    sent[:, :diag_rows, :] = diag.reshape(poles, diag_rows, width)
    sent[:, diag_rows:, :] = off_term.reshape(poles, off_rows, width)


def add_poles(cols, diag_rows, held, diag, off):
    total = jnp.sum(held[...], axis=0)
    for c in range(cols):
        diag[c] = total[:diag_rows]
    off[...] = total[diag_rows:]


def add_cols(poles, diag_rows, held, off, sent):
    total = jnp.sum(held[...], axis=0)
    for p in range(poles):
        sent[p, :diag_rows] = total
        sent[p, diag_rows:] = off[...]


def per_device(factor, green, diag_inv, pole_weight, structure, widths):
    poles, rows, cols = (lax.axis_size(name) for name in ("pole", "row", "col"))
    rows_here, node_count, width = factor.shape[2:]
    cols_here = green.shape[3]
    block_rows = rows_here * rows // structure.shape[1]
    diag_rows, off_rows = width // poles, cols_here // poles
    f32 = jnp.float32

    lower = factor[0].transpose(2, 0, 1, 3).reshape(node_count, 2 * rows_here, width)
    packed = jnp.concatenate([green[0, 0], green[0, 1]], axis=1)
    packed = jnp.broadcast_to(packed[None], (node_count, rows_here, 2 * cols_here))
    held = lax.all_to_all(jnp.concatenate([lower, packed], axis=1), "row", 0, 0, tiled=True)

    sent = pl.pallas_call(
        lambda *refs: compute(cols_here, rows_here, block_rows, poles, *refs),
        out_shape=jax.ShapeDtypeStruct((poles, diag_rows + off_rows, width), f32),
        in_specs=[VMEM, VMEM, SMEM, SMEM, SMEM],
        out_specs=VMEM,
        name="compute",
    )(held, diag_inv[0, :, 0], pole_weight, structure.T, widths)
    held = lax.all_to_all(sent, "pole", 0, 0, tiled=True)
    sent, off = pl.pallas_call(
        lambda *refs: add_poles(cols, diag_rows, *refs),
        out_shape=(
            jax.ShapeDtypeStruct((cols, diag_rows, width), f32),
            jax.ShapeDtypeStruct((off_rows, width), f32),
        ),
        in_specs=[VMEM],
        out_specs=(VMEM, VMEM),
        name="add_poles",
    )(held)
    held = lax.all_to_all(sent, "col", 0, 0, tiled=True)
    sent = pl.pallas_call(
        lambda *refs: add_cols(poles, diag_rows, *refs),
        out_shape=jax.ShapeDtypeStruct((poles, diag_rows + off_rows, width), f32),
        in_specs=[VMEM, VMEM],
        out_specs=VMEM,
        name="add_cols",
    )(held, off)
    held = lax.all_to_all(sent, "pole", 0, 0, tiled=True)
    density_diag = held[:, :diag_rows].reshape(1, width, width)
    density_off = held[:, diag_rows:].reshape(1, cols_here, width).transpose(0, 2, 1)
    return (density_off, density_diag)


def solution(mesh):
    placed = (
        P("pole", None, "row", None, None),
        P("pole", None, "row", "col"),
        P("pole", None, "row", None, None),
        P("pole", None),
        P(),
        P(),
    )
    return jax.shard_map(
        per_device,
        mesh=mesh,
        in_specs=placed,
        out_specs=(P("row", None, "col"), P("row", None, None)),
        check_vma=False,
    )
```

time: 689 us -> 93.8 us (0.14)
  waiting for transfers between devices: 617 us -> 0 us
  blocking collectives: 23 us -> 83.8 us
  between operations: 14.2 us -> 0.65 us
  matrix products: 11.3 us -> 0 us
  starting transfers between devices: 11 us -> 0 us
    psum x1 -> x0, waiting for transfers between devices: 477 us -> none  [per_device(): density_diag = lax.psum(diag_term, ('pole', 'col'))]
    unnamed x3 -> x0, waiting for transfers between devices: 131 us -> none
    all_to_all x0 -> x4, blocking collectives: none -> 83.8 us  [the longest x2 30.9 us: per_device(): held = lax.all_to_all(sent, 'pole', 0, 0, tiled=True)]
    psum x1 -> x0, blocking collectives: 23 us -> none  [per_device(): density_off = lax.psum(off_term, 'pole')]
    dot_general x8 -> x0, matrix products: 11.3 us -> none  [contract(): jnp.einsum(form, left, right, precision=highest, preferred_element_type=j...]
    all_to_all x1 -> x0, starting transfers between devices: 10.9 us -> none  [per_device(): lax.all_to_all(lower_here, 'row', split_axis=2, concat_axis=1, tiled=True)]
    all_to_all x1 -> x0, waiting for transfers between devices: 9.24 us -> none  [per_device(): lax.all_to_all(lower_here, 'row', split_axis=2, concat_axis=1, tiled=True)]
  transfers between devices with their start and end apart: 3 -> 0, of which waited for: 3 -> 0; matrix products, arithmetic and copies ran while one was open for 1% -> 0% of each run, Pallas kernels for 0% -> 0%
where the time goes in v1:
time: 93.8 us; the launch traced here: 93.1 us
  blocking collectives  83.8 us (89%)
  Pallas kernels  5.37 us (6%)
  local copies, waits for them, and re-layouts  3.22 us (3%)
    all_to_all x2, blocking collectives, per_device(): held = lax.all_to_all(sent, 'pole', 0, 0, tiled=True)  30.9 us
    all_to_all x1, blocking collectives, per_device(): lax.all_to_all(jnp.concatenate([lower, packed], axis=1), 'row', 0, 0, til...  26.9 us
    all_to_all x1, blocking collectives, per_device(): held = lax.all_to_all(sent, 'col', 0, 0, tiled=True)  26 us
    pallas_call x1, Pallas kernels, per_device(): pl.pallas_call(lambda *refs: compute(cols_here, rows_here, block_rows, po...  2.35 us

profile of v1, /device:TPU:1, one launch (start us, length us, event | category | flops | bytes accessed | tf_op | source)
XLA Modules:
  0.0 93.1 jit_solution(14851751876153708697)
XLA Ops:
  0.6 0.7 slice_bitcast_fusion.2
  1.4 1.2 %copy.8 = f32[16,2,32,128]{3,2,1,0:T(8,128)S(1)} copy(f32[16,2,32,128]{3,0,2,1:T(8,128)} %bitcast.16) | data formatting | bytes 1048576 | tf_op jit(solution)/shard_map/transpose | solution.py:92
  2.6 0.1 pad_maximum_fusion.1
  2.7 0.1 pad_maximum_fusion
  2.8 26.9 %all_to_all.20.refs_0_ = f32[16,96,128]{2,1,0:T(8,128)} all-to-all(f32[16,96,128]{2,1,0:T(8,128)S(1)} %pad_maximum_fusion), channel_id=1, replica_groups=mesh['pole'=8,'row'=16,'col'=8] {'row'}, dimensions={0} | all-to-all | bytes 1572864 | tf_op jit(solution)/shard_map/all_to_all | solution.py:95
  29.6 2.4 %compute.1 = f32[8,24,128]{2,1,0:T(8,128)} custom-call(f32[16,96,128]{2,1,0:T(8,128)} %all_to_all.20.refs_0_, f32[2,128,128]{2,1,0:T(8,128)} %bitcast.17, f32[1,2]{1,0:T(1,128)} %refs_2_.1, s32[8,16]{1,0:T(8,128)} %bitcast.19, s32[16]{0:T(128)} %refs_4_.1), custom_call_target="tpu_custom_call" | custom-call | tf_op jit(solution)/shard_map/compute/pallas_call | solution.py:97
  32.0 20.2 %all_to_all.21.refs_0_ = f32[8,24,128]{2,1,0:T(8,128)} all-to-all(f32[8,24,128]{2,1,0:T(8,128)} %compute.1), channel_id=1, replica_groups=mesh['pole'=8,'row'=16,'col'=8] {'pole'}, dimensions={0} | all-to-all | bytes 196608 | tf_op jit(solution)/shard_map/all_to_all | solution.py:104
  52.2 1.5 %add_poles.1 = (f32[8,16,128]{2,1,0:T(8,128)}, f32[8,128]{1,0:T(8,128)}) custom-call(f32[8,24,128]{2,1,0:T(8,128)} %all_to_all.21.refs_0_), custom_call_target="tpu_custom_call" | custom-call | tf_op jit(solution)/shard_map/add_poles/pallas_call | solution.py:105
  53.7 26.0 %all_to_all.22.refs_0_ = f32[8,16,128]{2,1,0:T(8,128)} all-to-all(f32[8,16,128]{2,1,0:T(8,128)} %get-tuple-element.4), channel_id=1, replica_groups=mesh['pole'=8,'row'=16,'col'=8] {'col'}, dimensions={0} | all-to-all | bytes 131072 | tf_op jit(solution)/shard_map/all_to_all | solution.py:115
  79.7 1.5 %add_cols.1 = f32[8,24,128]{2,1,0:T(8,128)} custom-call(f32[8,16,128]{2,1,0:T(8,128)} %all_to_all.22.refs_0_, f32[8,128]{1,0:T(8,128)} %get-tuple-element.5.refs_1_), custom_call_target="tpu_custom_call" | custom-call | tf_op jit(solution)/shard_map/add_cols/pallas_call | solution.py:116
  81.2 10.7 %all_to_all.23 = f32[8,24,128]{2,1,0:T(8,128)S(1)} all-to-all(f32[8,24,128]{2,1,0:T(8,128)} %add_cols.1), channel_id=1, replica_groups=mesh['pole'=8,'row'=16,'col'=8] {'pole'}, dimensions={0} | all-to-all | bytes 196608 | tf_op jit(solution)/shard_map/all_to_all | solution.py:123
  91.9 0.6 slice_bitcast_fusion
  92.5 0.6 slice.17
  (1 shorter events, 0.0 us)

commit v2 on v1

v2 whole, which is shorter than its diff:
```python
import jax
import jax.numpy as jnp
from jax import lax
from jax.experimental import pallas as pl
from jax.experimental.pallas import tpu as pltpu
from jax.sharding import Mesh, PartitionSpec as P

LIMIT = 8 * 1024 * 1024
PACK_LIMIT = 60 * 1024 * 1024
ANY = pl.BlockSpec(memory_space=pl.ANY)
VMEM = pl.BlockSpec(memory_space=pltpu.VMEM)
SMEM = pl.BlockSpec(memory_space=pltpu.SMEM)
PARAMS = pltpu.CompilerParams(vmem_limit_bytes=LIMIT)


def split(value):
    high = value.astype(jnp.bfloat16)
    return high, (value - high.astype(jnp.float32)).astype(jnp.bfloat16)


def product(left, right):
    left_high, left_low = split(left)
    right_high, right_low = split(right)

    def one(a, b):
        return lax.dot_general(a, b, (((0,), (0,)), ((), ())), preferred_element_type=jnp.float32)

    return one(left_high, right_high) + (one(left_high, right_low) + one(left_low, right_high))


def pack(rows_here, factor, green, weight, structure, widths, sent, scalars, held_green, sems):
    node_here = lax.axis_index("row")
    core = lax.axis_index("core")
    nodes, _, width = sent.shape
    copies = [
        pltpu.make_async_copy(factor.at[0, core, :, node, :], sent.at[node, pl.ds(0, rows_here), :], sems.at[node])
        for node in range(nodes)
    ]
    load = pltpu.make_async_copy(green.at[0], held_green, sems.at[nodes])
    load.start()
    for copy in copies:
        copy.start()
    scalars[0:1, :] = jnp.full((1, width), weight[0, 0])
    scalars[1:2, :] = jnp.full((1, width), weight[0, 1])
    scalars[2:3, :] = jnp.full((1, width), widths[node_here].astype(jnp.float32))
    for block in range(structure.shape[0]):
        scalars[8 + block : 9 + block, :] = jnp.full((1, width), structure[block, node_here].astype(jnp.float32))
    load.wait()
    packed = jnp.concatenate([held_green[0], held_green[1]], axis=1)
    for node in range(nodes):
        sent[node, rows_here:, :] = packed
    for copy in copies:
        copy.wait()


def compute(sizes, mine, other, inverse, scalars, sent):
    cols_here, rows_here, block_rows, poles = sizes
    col = 2 * lax.axis_index("zh") + lax.axis_index("core")
    first_core = lax.axis_index("core") == 0
    owners, _, width = mine.shape
    real_weight, imag_weight, count = scalars[0:1, :], scalars[1:2, :], scalars[2:3, :]

    def part_of(held, start, size):
        return held[pl.ds(start, size), :rows_here, :].reshape(size * rows_here, width)

    def both(start, size, axis):
        one, two = part_of(mine, start, size), part_of(other, start, size)
        return jnp.concatenate([jnp.where(first_core, one, two), jnp.where(first_core, two, one)], axis=axis)

    green = []
    for r in range(owners):
        block = 8 + r * rows_here // block_rows
        green.append(mine[r, rows_here:, :] * scalars[block : block + 1, :])
    parts = product(jnp.concatenate(green, axis=0), both(0, owners, 1))
    real_part = parts[cols_here:, width:] - parts[:cols_here, :width]
    imag_part = -(parts[cols_here:, :width] + parts[:cols_here, width:])

    def keep(rows, axis):
        return (lax.broadcasted_iota(jnp.int32, (rows, width), axis).astype(jnp.float32) < count).astype(jnp.float32)

    keep_lane = keep(cols_here, 1) * scalars[pl.ds(8 + col * cols_here // block_rows, 1), :]
    off_term = (real_weight * imag_part + imag_weight * real_part) * keep_lane
    rest = (real_weight * real_part - imag_weight * imag_part) * keep_lane
    span = cols_here // rows_here
    diag = product(jnp.concatenate([off_term, rest], axis=0), both(col * span, span, 0))
    first = (col == 0).astype(jnp.float32)
    diag = (first * (real_weight * inverse[1] + imag_weight * inverse[0]) - diag) * (keep(width, 1) * keep(width, 0))
    diag_rows, off_rows = width // poles, cols_here // poles
    sent[:, :diag_rows, :] = diag.reshape(poles, diag_rows, width)
    sent[:, diag_rows:, :] = off_term.reshape(poles, off_rows, width)


def add_poles(copies, diag_rows, held, diag, off):
    total = jnp.sum(held[...], axis=0)
    for c in range(copies):
        diag[c] = total[:diag_rows]
    off[...] = total[diag_rows:]


def add_cols(copies, diag_rows, held, off, sent):
    total = jnp.sum(held[...], axis=0)
    for p in range(copies):
        sent[p, :diag_rows] = total
        sent[p, diag_rows:] = off[...]


def deliver(diag_rows, held, diag, off, sems):
    copies = [
        pltpu.make_async_copy(held.at[:, :diag_rows, :], diag, sems.at[0]),
        pltpu.make_async_copy(held.at[:, diag_rows:, :], off, sems.at[1]),
    ]
    for copy in copies:
        copy.start()
    for copy in copies:
        copy.wait()


def per_device(factor, green, diag_inv, pole_weight, structure, widths):
    poles, rows, chips, cores = (lax.axis_size(name) for name in ("pole", "row", "zh", "core"))
    rows_here, node_count, width = factor.shape[2:]
    cols_here = green.shape[3]
    block_rows = rows_here * rows // structure.shape[1]
    diag_rows, off_rows = width // poles, cols_here // poles
    sent_rows = diag_rows + off_rows
    f32 = jnp.float32

    sent, scalars = pl.pallas_call(
        lambda *refs: pack(rows_here, *refs),
        out_shape=(
            jax.ShapeDtypeStruct((node_count, 2 * rows_here, width), f32),
            jax.ShapeDtypeStruct((8 + structure.shape[1], width), f32),
        ),
        in_specs=[ANY, ANY, SMEM, SMEM, SMEM],
        out_specs=(VMEM, VMEM),
        scratch_shapes=[
            pltpu.VMEM((2, rows_here, cols_here), f32),
            pltpu.SemaphoreType.DMA((node_count + 1,)),
        ],
        compiler_params=pltpu.CompilerParams(vmem_limit_bytes=PACK_LIMIT),
        name="pack",
    )(factor, green, pole_weight, structure.T, widths)
    mine = lax.all_to_all(sent, "row", 0, 0, tiled=True)
    other = lax.ppermute(mine, "core", [(0, 1), (1, 0)])
    sent = pl.pallas_call(
        lambda *refs: compute((cols_here, rows_here, block_rows, poles), *refs),
        out_shape=jax.ShapeDtypeStruct((poles, sent_rows, width), f32),
        in_specs=[VMEM, VMEM, VMEM, VMEM],
        out_specs=VMEM,
        compiler_params=PARAMS,
        name="compute",
    )(mine, other, diag_inv[0, :, 0], scalars)
    held = lax.all_to_all(sent, "pole", 0, 0, tiled=True)
    sent, off = pl.pallas_call(
        lambda *refs: add_poles(chips * cores, diag_rows, *refs),
        out_shape=(
            jax.ShapeDtypeStruct((chips * cores, diag_rows, width), f32),
            jax.ShapeDtypeStruct((off_rows, width), f32),
        ),
        in_specs=[VMEM],
        out_specs=(VMEM, VMEM),
        compiler_params=PARAMS,
        name="add_poles",
    )(held)
    held = lax.all_to_all(sent, ("zh", "core"), 0, 0, tiled=True)
    sent = pl.pallas_call(
        lambda *refs: add_cols(poles, diag_rows, *refs),
        out_shape=jax.ShapeDtypeStruct((poles, sent_rows, width), f32),
        in_specs=[VMEM, VMEM],
        out_specs=VMEM,
        compiler_params=PARAMS,
        name="add_cols",
    )(held, off)
    held = lax.all_to_all(sent, "pole", 0, 0, tiled=True)
    diag, off = pl.pallas_call(
        lambda *refs: deliver(diag_rows, *refs),
        out_shape=(
            jax.ShapeDtypeStruct((poles, diag_rows, width), f32),
            jax.ShapeDtypeStruct((poles, off_rows, width), f32),
        ),
        in_specs=[VMEM],
        out_specs=(ANY, ANY),
        scratch_shapes=[pltpu.SemaphoreType.DMA((2,))],
        compiler_params=PARAMS,
        name="deliver",
    )(held)
    density_diag = diag.reshape(1, width, width)
    density_off = off.reshape(1, cols_here, width).transpose(0, 2, 1)
    return (density_off, density_diag)


def solution(mesh):
    poles, rows, cols = (mesh.shape[name] for name in ("pole", "row", "col"))
    finer = Mesh(mesh.devices.reshape(poles, rows, cols // 2, 2), ("pole", "row", "zh", "core"))
    col = ("zh", "core")
    placed = (
        P("pole", None, "row", None, None),
        P("pole", None, "row", col),
        P("pole", None, "row", None, None),
        P("pole", None),
        P(),
        P(),
    )
    return jax.shard_map(
        per_device,
        mesh=finer,
        in_specs=placed,
        out_specs=(P("row", None, col), P("row", None, None)),
        check_vma=False,
    )
```

time: 93.8 us -> 85.4 us (0.910)
  blocking collectives: 83.8 us -> 68.4 us
  starting transfers between devices: 0 us -> 10.4 us
  local copies, waits for them, and re-layouts: 3.22 us -> 0.01 us
  Pallas kernels: 5.37 us -> 3.83 us
  waiting for transfers between devices: 0 us -> 1.51 us
    ppermute x0 -> x1, starting transfers between devices: none -> 10.4 us  [per_device(): other = lax.ppermute(mine, 'core', [(0, 1), (1, 0)])]
    all_to_all x2, blocking collectives: 30.9 us -> 21.4 us  [per_device(): held = lax.all_to_all(sent, 'pole', 0, 0, tiled=True)]
    all_to_all x2, blocking collectives: 52.8 us -> 47 us  [the longest x1 24.1 us: per_device(): held = lax.all_to_all(sent, ('zh', 'core'), 0, 0, tiled=True)]
    transpose x2 -> x0, local copies, waits for them, and re-layouts: 1.83 us -> none  [the longest x1 1.21 us: per_device(): factor[0].transpose(2, 0, 1, 3).reshape(node_count, 2 * rows_here, width)]
    ppermute x0 -> x1, waiting for transfers between devices: none -> 1.51 us  [per_device(): other = lax.ppermute(mine, 'core', [(0, 1), (1, 0)])]
    pallas_call x1, Pallas kernels: 1.48 us -> 0.01 us  [per_device(): pl.pallas_call(lambda *refs: add_cols(poles, diag_rows, *refs), out_shape...]
    pallas_call x2 -> x4, Pallas kernels: 3.89 us -> 3.82 us  [the longest x1 2.59 us: per_device(): pl.pallas_call(lambda *refs: pack(rows_here, *refs), out_shape=(jax.Shape...]
  transfers between devices with their start and end apart: 0 -> 1, of which waited for: 0 -> 1; matrix products, arithmetic and copies ran while one was open for 0% -> 0% of each run, Pallas kernels for 0% -> 0%
where the time goes in v2:
time: 85.4 us; the launch traced here: 84.9 us
  blocking collectives  68.4 us (80%)
  starting transfers between devices  10.4 us (12%)
  Pallas kernels  3.83 us (4%)
  waiting for transfers between devices  1.51 us (2%)
    all_to_all x1, blocking collectives, per_device(): held = lax.all_to_all(sent, ('zh', 'core'), 0, 0, tiled=True)  24.1 us
    all_to_all x1, blocking collectives, per_device(): mine = lax.all_to_all(sent, 'row', 0, 0, tiled=True)  23 us
    all_to_all x2, blocking collectives, per_device(): held = lax.all_to_all(sent, 'pole', 0, 0, tiled=True)  21.4 us
    ppermute x1, starting transfers between devices, per_device(): other = lax.ppermute(mine, 'core', [(0, 1), (1, 0)])  10.4 us
    pallas_call x1, Pallas kernels, per_device(): pl.pallas_call(lambda *refs: pack(rows_here, *refs), out_shape=(jax.Shape...  2.59 us
  transfers between devices with their start and end apart: 1, of which 1 were waited for; matrix products, arithmetic and copies ran while one was open for 0% of the time, Pallas kernels for 0%

profile of v2, /device:TPU:1, one launch (start us, length us, event | category | flops | bytes accessed | tf_op | source)
XLA Modules:
  0.0 84.9 jit_solution(10471389716366312557)
XLA Ops:
  0.6 2.6 %pack.1 = (f32[16,64,128]{2,1,0:T(8,128)}, f32[16,128]{1,0:T(8,128)}) custom-call(f32[1,2,32,16,128]{4,3,2,1,0:T(8,128)} %refs_0_.1, f32[1,2,32,64]{3,2,1,0:T(8,128)} %refs_1_.1, f32[1,2]{1,0:T(1,128)} %refs_2_.1, s32[8,16]{1,0:T(8,128)} %bitcast.7, s32[16]{0:T(128)} %refs_4_.1), custom_call_target="tpu_custom_call" | custom-call | tf_op jit(solution)/shard_map/pack/pallas_call | solution.py:127
  3.2 0.0 copy-start
  3.2 0.0 copy-start.1
  3.3 23.0 %all_to_all.20.refs_0_ = f32[16,64,128]{2,1,0:T(8,128)S(1)} all-to-all(f32[16,64,128]{2,1,0:T(8,128)} %get-tuple-element.8), channel_id=1, replica_groups=mesh['pole'=8,'row'=16,'zh'=4,'core'=2] {'row'}, dimensions={0} | all-to-all | bytes 1048576 | tf_op jit(solution)/shard_map/all_to_all | solution.py:142
  26.2 10.4 %collective-permute-start = (f32[16,64,128]{2,1,0:T(8,128)S(1)}, f32[16,64,128]{2,1,0:T(8,128)S(1)}, u32[]{:S(2)}, u32[]{:S(2)}) collective-permute-start(f32[16,64,128]{2,1,0:T(8,128)S(1)} %all_to_all.20.refs_0_), channel_id=1, source_target_pairs={{0,1},{1,0},{2,3},{3,2},{4,5},{5,4},{6,7},{7,6},{8,9},{9,8},{10,11... | collective-permute-start | bytes 1572872 | tf_op jit(solution)/shard_map/ppermute | solution.py:143
  36.6 1.5 %collective-permute-done.refs_1_ = f32[16,64,128]{2,1,0:T(8,128)S(1)} collective-permute-done((f32[16,64,128]{2,1,0:T(8,128)S(1)}, f32[16,64,128]{2,1,0:T(8,128)S(1)}, u32[]{:S(2)}, u32[]{:S(2)}) %collective-permute-start) | collective-permute-done | bytes 524320 | tf_op jit(solution)/shard_map/ppermute | solution.py:143
  38.2 0.0 copy-done
  38.2 0.0 copy-done.1
  38.2 0.6 compute.1
  38.7 11.6 %all_to_all.21.refs_0_ = f32[8,24,128]{2,1,0:T(8,128)S(1)} all-to-all(f32[8,24,128]{2,1,0:T(8,128)S(1)} %compute.1), channel_id=1, replica_groups=mesh['pole'=8,'row'=16,'zh'=4,'core'=2] {'pole'}, dimensions={0} | all-to-all | bytes 196608 | tf_op jit(solution)/shard_map/all_to_all | solution.py:152
  50.3 24.1 %all_to_all.22.refs_0_ = f32[8,16,128]{2,1,0:T(8,128)S(1)} all-to-all(f32[8,16,128]{2,1,0:T(8,128)S(1)} %get-tuple-element.10), channel_id=1, replica_groups=mesh['pole'=8,'row'=16,'zh'=4,'core'=2] {'zh','core'}, dimensions={0} | all-to-all | bytes 131072 | tf_op jit(solution)/shard_map/all_to_all | solution.py:164
  74.4 9.8 %all_to_all.23.refs_0_ = f32[8,24,128]{2,1,0:T(8,128)S(1)} all-to-all(f32[8,24,128]{2,1,0:T(8,128)S(1)} %add_cols.1), channel_id=1, replica_groups=mesh['pole'=8,'row'=16,'zh'=4,'core'=2] {'pole'}, dimensions={0} | all-to-all | bytes 196608 | tf_op jit(solution)/shard_map/all_to_all | solution.py:173
  84.2 0.7 deliver.1
  (2 shorter events, 0.0 us)
Async XLA Ops:
  3.2 34.9 %copy-start = (f32[1,2,1,128,128]{4,3,2,1,0:T(8,128)S(1)}, f32[1,2,1,128,128]{4,3,2,1,0:T(8,128)}, u32[]{:S(2)}) copy-start(f32[1,2,1,128,128]{4,3,2,1,0:T(8,128)} %param.8) | copy-start | bytes 393220
  3.2 34.9 %copy-start.1 = (f32[16,128]{1,0:T(8,128)S(1)}, f32[16,128]{1,0:T(8,128)}, u32[]{:S(2)}) copy-start(f32[16,128]{1,0:T(8,128)} %get-tuple-element.9.refs_3_) | copy-start | bytes 24580
  26.2 11.9 %collective-permute-start = (f32[16,64,128]{2,1,0:T(8,128)S(1)}, f32[16,64,128]{2,1,0:T(8,128)S(1)}, u32[]{:S(2)}, u32[]{:S(2)}) collective-permute-start(f32[16,64,128]{2,1,0:T(8,128)S(1)} %all_to_all.20.refs_0_), channel_id=1, source_target_pairs={{0,1},{1,0},{2,3},{3,2},{4,5},{5,4},{6,7},{7,6},{8,9},{9,8},{10,11... | collective-permute-start | bytes 1572872 | tf_op jit(solution)/shard_map/ppermute | solution.py:143

commit v3 on v2

v3 whole, which is shorter than its diff:
```python
import jax
import jax.numpy as jnp
from jax import lax
from jax.experimental import pallas as pl
from jax.experimental.pallas import tpu as pltpu
from jax.sharding import Mesh, PartitionSpec as P

LIMIT = 8 * 1024 * 1024
ANY = pl.BlockSpec(memory_space=pl.ANY)
VMEM = pl.BlockSpec(memory_space=pltpu.VMEM)
SMEM = pl.BlockSpec(memory_space=pltpu.SMEM)


def split(value):
    high = value.astype(jnp.bfloat16)
    return high, (value - high.astype(jnp.float32)).astype(jnp.bfloat16)


def product(left, right):
    left_high, left_low = split(left)
    right_high, right_low = split(right)

    def one(a, b):
        return lax.dot_general(a, b, (((0,), (0,)), ((), ())), preferred_element_type=jnp.float32)

    return one(left_high, right_high) + (one(left_high, right_low) + one(left_low, right_high))


def pack(rows_here, factor, green, sent, held_green, sems):
    core = lax.axis_index("core")
    nodes = sent.shape[0]
    load = pltpu.make_async_copy(green.at[0], held_green, sems.at[nodes])
    load.start()
    copies = [
        pltpu.make_async_copy(factor.at[0, core, :, node, :], sent.at[node, pl.ds(0, rows_here), :], sems.at[node])
        for node in range(nodes)
    ]
    for copy in copies:
        copy.start()
    load.wait()
    packed = jnp.concatenate([held_green[0], held_green[1]], axis=1)
    for node in range(nodes):
        sent[node, rows_here:, :] = packed
    for copy in copies:
        copy.wait()


def spell(weight, structure, widths, scalars):
    node_here = lax.axis_index("row")
    width = scalars.shape[1]
    scalars[0:1, :] = jnp.full((1, width), weight[0, 0])
    scalars[1:2, :] = jnp.full((1, width), weight[0, 1])
    scalars[2:3, :] = jnp.full((1, width), widths[node_here].astype(jnp.float32))
    scalars[3:8, :] = jnp.zeros((5, width), jnp.float32)
    for block in range(structure.shape[0]):
        scalars[8 + block : 9 + block, :] = jnp.full((1, width), structure[block, node_here].astype(jnp.float32))


def compute(sizes, mine, other, inverse, scalars, sent):
    cols_here, rows_here, block_rows, poles = sizes
    chip = lax.axis_index("zh")
    first_core = lax.axis_index("core") == 0
    owners, _, width = mine.shape
    real_weight, imag_weight, count = scalars[0:1, :], scalars[1:2, :], scalars[2:3, :]

    def part_of(held, start, size):
        return held[pl.ds(start, size), :rows_here, :].reshape(size * rows_here, width)

    def both(start, size, axis):
        one, two = part_of(mine, start, size), part_of(other, start, size)
        return jnp.concatenate([jnp.where(first_core, one, two), jnp.where(first_core, two, one)], axis=axis)

    def green_of(held):
        rows = []
        for r in range(owners):
            block = 8 + r * rows_here // block_rows
            rows.append(held[r, rows_here:, :] * scalars[block : block + 1, :])
        return jnp.concatenate(rows, axis=0)

    def keep(rows, axis):
        return (lax.broadcasted_iota(jnp.int32, (rows, width), axis).astype(jnp.float32) < count).astype(jnp.float32)

    parts = product(jnp.concatenate([green_of(mine), green_of(other)], axis=1), both(0, owners, 1))
    keep_lane = keep(cols_here, 1)
    span = cols_here // rows_here
    left, right = [], []
    for c in range(2):
        real_rows = parts[2 * c * cols_here : (2 * c + 1) * cols_here]
        imag_rows = parts[(2 * c + 1) * cols_here : (2 * c + 2) * cols_here]
        real_part = imag_rows[:, width:] - real_rows[:, :width]
        imag_part = -(imag_rows[:, :width] + real_rows[:, width:])
        core = lax.axis_index("core")
        col = 2 * chip + (core if c == 0 else 1 - core)
        kept = keep_lane * scalars[pl.ds(8 + col * cols_here // block_rows, 1), :]
        left.append((real_weight * imag_part + imag_weight * real_part) * kept)
        left.append((real_weight * real_part - imag_weight * imag_part) * kept)
        right.append(both(col * span, span, 0))
    diag = product(jnp.concatenate(left, axis=0), jnp.concatenate(right, axis=0))
    first = (chip == 0).astype(jnp.float32)
    diag = (first * (real_weight * inverse[1] + imag_weight * inverse[0]) - diag) * (keep(width, 1) * keep(width, 0))
    diag_rows, off_rows = width // poles, cols_here // poles
    sent[:, :diag_rows, :] = diag.reshape(poles, diag_rows, width)
    sent[:, diag_rows:, :] = left[0].reshape(poles, off_rows, width)


def add_poles(copies, diag_rows, held, diag, off):
    total = jnp.sum(held[...], axis=0)
    for c in range(copies):
        diag[c] = total[:diag_rows]
    off[...] = total[diag_rows:]


def add_cols(copies, diag_rows, held, off, sent):
    total = jnp.sum(held[...], axis=0)
    for p in range(copies):
        sent[p, :diag_rows] = total
        sent[p, diag_rows:] = off[...]


def deliver(diag_rows, held, diag, off, sems):
    copies = [
        pltpu.make_async_copy(held.at[:, :diag_rows, :], diag, sems.at[0]),
        pltpu.make_async_copy(held.at[:, diag_rows:, :], off, sems.at[1]),
    ]
    for copy in copies:
        copy.start()
    for copy in copies:
        copy.wait()


def per_device(factor, green, diag_inv, pole_weight, structure, widths):
    poles, rows, chips = (lax.axis_size(name) for name in ("pole", "row", "zh"))
    rows_here, node_count, width = factor.shape[2:]
    cols_here = green.shape[3]
    block_rows = rows_here * rows // structure.shape[1]
    diag_rows, off_rows = width // poles, cols_here // poles
    sent_rows = diag_rows + off_rows
    f32 = jnp.float32

    def call(body, name, out_shape, in_specs, out_specs, scratch_shapes=()):
        with jax.named_scope(name):
            return pl.pallas_call(
                body,
                out_shape=out_shape,
                in_specs=in_specs,
                out_specs=out_specs,
                scratch_shapes=scratch_shapes,
                compiler_params=pltpu.CompilerParams(vmem_limit_bytes=LIMIT),
                cost_estimate=pl.CostEstimate(flops=1000000, bytes_accessed=1000000, transcendentals=0),
                name=name,
            )

    def shape(*dims):
        return jax.ShapeDtypeStruct(dims, f32)

    def exchange(name, value, axis):
        with jax.named_scope(name):
            return lax.all_to_all(value, axis, 0, 0, tiled=True)

    sent = call(
        lambda *refs: pack(rows_here, *refs),
        "pack",
        shape(node_count, 2 * rows_here, width),
        [ANY, ANY],
        VMEM,
        [
            pltpu.VMEM((2, rows_here, cols_here), f32),
            pltpu.SemaphoreType.DMA((node_count + 1,)),
        ],
    )(pltpu.with_memory_space_constraint(factor, pltpu.HBM), pltpu.with_memory_space_constraint(green, pltpu.HBM))
    scalars = call(spell, "spell", shape(8 + structure.shape[1], width), [SMEM] * 3, VMEM)(
        pole_weight, structure.T, widths
    )
    mine = exchange("over_row", sent, "row")
    with jax.named_scope("swap"):
        other = lax.ppermute(mine, "core", [(0, 1), (1, 0)])
    sent = call(
        lambda *refs: compute((cols_here, rows_here, block_rows, poles), *refs),
        "compute",
        shape(poles, sent_rows, width),
        [VMEM] * 4,
        VMEM,
    )(mine, other, diag_inv[0, :, 0], scalars)
    held = exchange("over_pole", sent, "pole")
    sent, off = call(
        lambda *refs: add_poles(chips, diag_rows, *refs),
        "add_poles",
        (shape(chips, diag_rows, width), shape(off_rows, width)),
        [VMEM],
        (VMEM, VMEM),
    )(held)
    held = exchange("over_chips", sent, "zh")
    sent = call(
        lambda *refs: add_cols(poles, diag_rows, *refs), "add_cols", shape(poles, sent_rows, width), [VMEM, VMEM], VMEM
    )(held, off)
    held = exchange("back_over_pole", sent, "pole")
    diag, off = call(
        lambda *refs: deliver(diag_rows, *refs),
        "deliver",
        (shape(poles, diag_rows, width), shape(poles, off_rows, width)),
        [VMEM],
        (ANY, ANY),
        [pltpu.SemaphoreType.DMA((2,))],
    )(held)
    density_diag = diag.reshape(1, width, width)
    density_off = off.reshape(1, cols_here, width).transpose(0, 2, 1)
    return (density_off, density_diag)


def solution(mesh):
    poles, rows, cols = (mesh.shape[name] for name in ("pole", "row", "col"))
    finer = Mesh(mesh.devices.reshape(poles, rows, cols // 2, 2), ("pole", "row", "zh", "core"))
    col = ("zh", "core")
    placed = (
        P("pole", None, "row", None, None),
        P("pole", None, "row", col),
        P("pole", None, "row", None, None),
        P("pole", None),
        P(),
        P(),
    )
    return jax.shard_map(
        per_device,
        mesh=finer,
        in_specs=placed,
        out_specs=(P("row", None, col), P("row", None, None)),
        check_vma=False,
    )
```

time: 85.4 us -> 83.1 us (0.973)
  the two profiles are of different devices: /device:TPU:1 before, /device:TPU:2 now
where the time goes in v3:
time: 83.1 us; the launch traced here: 82.7 us
  blocking collectives  75.7 us (91%)
  Pallas kernels  3.1 us (4%)
  starting transfers between devices  2.04 us (2%)
  waiting for transfers between devices  1.2 us (1%)
    all_to_all x4, blocking collectives, exchange(): return lax.all_to_all(value, axis, 0, 0, tiled=True)  75.7 us
    ppermute x1, starting transfers between devices, per_device(): other = lax.ppermute(mine, 'core', [(0, 1), (1, 0)])  2.04 us
  transfers between devices with their start and end apart: 1, of which 1 were waited for; matrix products, arithmetic and copies ran while one was open for 0% of the time, Pallas kernels for 1%

profile of v3, /device:TPU:2, one launch (start us, length us, event | category | flops | bytes accessed | tf_op | source)
XLA Modules:
  0.0 82.7 jit_solution(1993268639375202233)
XLA Ops:
  0.6 1.1 %pack.1 = f32[16,64,128]{2,1,0:T(8,128)S(1)} custom-call(f32[1,2,32,16,128]{4,3,2,1,0:T(8,128)} %refs_0_.1, f32[1,2,32,64]{3,2,1,0:T(8,128)} %refs_1_.1), custom_call_target="tpu_custom_call" | custom-call | flops 1000000 | bytes 1000000 | tf_op jit(solution)/shard_map/pack/pallas_call | solution.py:160
  1.7 0.0 copy-start.1
  1.7 0.0 copy-start
  1.7 27.6 %all_to_all.20.refs_0_ = f32[16,64,128]{2,1,0:T(8,128)S(1)} all-to-all(f32[16,64,128]{2,1,0:T(8,128)S(1)} %pack.1), channel_id=1, replica_groups=mesh['pole'=8,'row'=16,'zh'=4,'core'=2] {'row'}, dimensions={0} | all-to-all | bytes 1048576 | tf_op jit(solution)/shard_map/over_row/all_to_all | solution.py:158
  29.3 0.0 copy-start.2
  29.4 0.0 copy-start.3
  29.4 2.0 %collective-permute-start = (f32[16,64,128]{2,1,0:T(8,128)S(1)}, f32[16,64,128]{2,1,0:T(8,128)S(1)}, u32[]{:S(2)}, u32[]{:S(2)}) collective-permute-start(f32[16,64,128]{2,1,0:T(8,128)S(1)} %all_to_all.20.refs_0_), channel_id=1, source_target_pairs={{0,1},{1,0},{2,3},{3,2},{4,5},{5,4},{6,7},{7,6},{8,9},{9,8},{10,11... | collective-permute-start | bytes 1572872 | tf_op jit(solution)/shard_map/swap/ppermute | solution.py:176
  31.4 0.0 copy-done.1
  31.4 0.0 copy-done.2
  31.4 0.0 copy-done.3
  31.4 0.6 spell.1.refs_3_
  32.1 1.2 %collective-permute-done.refs_1_ = f32[16,64,128]{2,1,0:T(8,128)S(1)} collective-permute-done((f32[16,64,128]{2,1,0:T(8,128)S(1)}, f32[16,64,128]{2,1,0:T(8,128)S(1)}, u32[]{:S(2)}, u32[]{:S(2)}) %collective-permute-start) | collective-permute-done | bytes 524320 | tf_op jit(solution)/shard_map/swap/ppermute | solution.py:176
  33.3 0.0 copy-done
  33.3 0.7 compute.1
  34.0 14.4 %all_to_all.21.refs_0_ = f32[8,24,128]{2,1,0:T(8,128)S(1)} all-to-all(f32[8,24,128]{2,1,0:T(8,128)S(1)} %compute.1), channel_id=1, replica_groups=mesh['pole'=8,'row'=16,'zh'=4,'core'=2] {'pole'}, dimensions={0} | all-to-all | bytes 196608 | tf_op jit(solution)/shard_map/over_pole/all_to_all | solution.py:158
  48.4 22.5 %all_to_all.22.refs_0_ = f32[4,16,128]{2,1,0:T(8,128)S(1)} all-to-all(f32[4,16,128]{2,1,0:T(8,128)S(1)} %get-tuple-element.6), channel_id=1, replica_groups=mesh['pole'=8,'row'=16,'zh'=4,'core'=2] {'zh'}, dimensions={0} | all-to-all | bytes 65536 | tf_op jit(solution)/shard_map/over_chips/all_to_all | solution.py:158
  70.9 11.2 %all_to_all.23.refs_0_ = f32[8,24,128]{2,1,0:T(8,128)S(1)} all-to-all(f32[8,24,128]{2,1,0:T(8,128)S(1)} %add_cols.1), channel_id=1, replica_groups=mesh['pole'=8,'row'=16,'zh'=4,'core'=2] {'pole'}, dimensions={0} | all-to-all | bytes 196608 | tf_op jit(solution)/shard_map/back_over_pole/all_to_all | solution.py:158
  82.1 0.7 deliver.1
  (2 shorter events, 0.0 us)
Async XLA Ops:
  1.7 29.7 %copy-start.1 = (s32[16,8]{0,1:T(8,128)S(1)}, s32[16,8]{0,1:T(8,128)}, u32[]{:S(2)}) copy-start(s32[16,8]{0,1:T(8,128)} %param.10) | copy-start | bytes 1540
  1.7 31.6 %copy-start = (f32[1,2,1,128,128]{4,3,2,1,0:T(8,128)S(1)}, f32[1,2,1,128,128]{4,3,2,1,0:T(8,128)}, u32[]{:S(2)}) copy-start(f32[1,2,1,128,128]{4,3,2,1,0:T(8,128)} %param.8) | copy-start | bytes 393220
  29.3 2.1 %copy-start.2 = (f32[1,2]{1,0:T(1,128)S(1)}, f32[1,2]{1,0:T(1,128)}, u32[]{:S(2)}) copy-start(f32[1,2]{1,0:T(1,128)} %weight.1) | copy-start | bytes 28
  29.4 2.1 %copy-start.3 = (s32[16]{0:T(128)S(1)}, s32[16]{0:T(128)}, u32[]{:S(2)}) copy-start(s32[16]{0:T(128)} %widths.1) | copy-start | bytes 196
  29.4 3.9 %collective-permute-start = (f32[16,64,128]{2,1,0:T(8,128)S(1)}, f32[16,64,128]{2,1,0:T(8,128)S(1)}, u32[]{:S(2)}, u32[]{:S(2)}) collective-permute-start(f32[16,64,128]{2,1,0:T(8,128)S(1)} %all_to_all.20.refs_0_), channel_id=1, source_target_pairs={{0,1},{1,0},{2,3},{3,2},{4,5},{5,4},{6,7},{7,6},{8,9},{9,8},{10,11... | collective-permute-start | bytes 1572872 | tf_op jit(solution)/shard_map/swap/ppermute | solution.py:176
